TPU v7x, 32 devices: a whole 2x2x4 slice. The times are simulated.
32 devices in a mesh: groups: 2 (over y), scen: 4 (over x, core), area: 4 (over z).
Axes of the slice: x: 2, y: 2, z: 4, core: 2. Of those that a mesh axis runs over, the one named last changes fastest.
Arguments:
- optimality_matrix_inverse: bfloat16 [8, 1024, 1024], P(('groups', 'area')), parts along dimension 0, as said below
- mean_requirement: bfloat16 [8, 1024, 16], P(('groups', 'area')), parts along dimension 0, may hold values from -6 to 6
- outcome_spread: bfloat16 [8, 1024, 2048], P(('groups', 'area'), None, 'scen'), parts along dimension 0, may hold values from -4 to 4
- outcome_likelihood_raw: float32 [256], P(('groups', 'scen')), parts along dimension 0, as said below
- prior_frontier_node_entries: bfloat16 [8, 32, 2048], P(('groups', 'area'), None, 'scen'), parts along dimension 0, may hold values from -6 to 6
- adjacent_regions: int32 [8, 4], P(('groups', 'area')), parts along dimension 0, may hold values from 0 to 3, as said below
- active_adjacent_entries: int32 [8], P(('groups', 'area')), parts along dimension 0, may hold values from 1 to 4
- linkage_entry_factor: float32 [8, 4], P(('groups', 'area')), parts along dimension 0, may hold values from 0.2 to 0.6
- plants_within_region: int32 [8], P(('groups', 'area')), parts along dimension 0, may hold values from 64 to 128
- inner_nodes_within_region: int32 [8], P(('groups', 'area')), parts along dimension 0, may hold values from 432 to 864
Outputs:
- commitment: float32 [8, 128, 16], P(('groups', 'area')), parts along dimension 0
- dual: float32 [8, 128, 2048], P(('groups', 'area'), None, 'scen'), parts along dimension 0
- boundary: float32 [8, 32, 2048], P(('groups', 'area'), None, 'scen'), parts along dimension 0
There are 2 independent parts, one for each index of `groups`. A program takes and returns all parts, laid end to end along the dimension named above; each array names one. Nothing has to cross between parts.
Inputs may be any that keep to these rules, and one draw needn't show every extreme that they name: `adjacent_regions`: each area's neighbours are other areas, never itself. `optimality_matrix_inverse`: each area's matrix has a positive diagonal. `outcome_likelihood_raw`: positive weights.
All inputs are finite; a program needn't handle non-finite values.
Results may differ from a plain program's by a relative error of at most 0.01.
Values may be sent and summed in bfloat16 or wider, within the bound.
A program may use at most 64 MiB of HBM per device.

v0:
```python
import functools

import jax
import jax.numpy as jnp
from jax import lax
from jax.experimental import pallas as pl
from jax.experimental.pallas import tpu as pltpu
from jax.sharding import PartitionSpec as P

GEN = 128
BND = 32
MAXN = 4
LANES = 128
CHUNKS = 4
MESH = pl.DeviceIdType.MESH
F32 = jnp.float32
BF16 = jnp.bfloat16

penalty = 1.0


def dot(a, b):
    return jnp.dot(a, b, preferred_element_type=F32)


def halves(x, axis):
    high = x.astype(BF16)
    low = (x - high.astype(F32)).astype(BF16)
    return jnp.concatenate([high, low], axis=axis)


def kernel(
    n_area,
    n_scen,
    raw_hbm,
    near_hbm,
    live_hbm,
    gain_hbm,
    plants_hbm,
    inner_hbm,
    matrix_ref,
    mean_ref,
    spread_ref,
    prior_ref,
    commit_ref,
    dual_ref,
    bound_ref,
    raw_ref,
    near_ref,
    live_ref,
    gain_ref,
    plants_ref,
    inner_ref,
    rows_buf,
    mean_buf,
    spread_buf,
    prior_buf,
    couple_buf,
    base_buf,
    sums_buf,
    sums_in,
    small_buf,
    edge_in,
    load_sem,
    word_sem,
    send_sem,
    recv_sem,
    scen_send,
    scen_recv,
):
    order = matrix_ref.shape[2]
    columns = spread_ref.shape[2]
    hours = mean_ref.shape[1]
    scen_here = raw_ref.shape[0]
    rows = GEN + BND
    groups = LANES // hours
    depth = order // CHUNKS
    wide = n_area * BND
    me = lax.axis_index("area")
    scen = lax.axis_index("scen")

    mine = pl.ds(pl.multiple_of(me * BND, BND), BND)
    my_small = pl.ds(pl.multiple_of(me * 8, 8), 8)
    loads = [
        pltpu.make_async_copy(prior_ref.at[0], prior_buf.at[mine], load_sem.at[0]),
        pltpu.make_async_copy(
            matrix_ref.at[0, pl.ds(0, GEN)], rows_buf.at[pl.ds(0, GEN)], load_sem.at[1]
        ),
        pltpu.make_async_copy(
            matrix_ref.at[0, pl.ds(order - BND, BND)], rows_buf.at[pl.ds(GEN, BND)], load_sem.at[2]
        ),
        pltpu.make_async_copy(mean_ref.at[0], mean_buf, load_sem.at[3]),
    ]
    for c in range(CHUNKS):
        part = pl.ds(c * depth, depth)
        loads.append(
            pltpu.make_async_copy(spread_ref.at[0, part], spread_buf.at[part], load_sem.at[4 + c])
        )
    pairs = (
        (raw_hbm, raw_ref),
        (near_hbm, near_ref),
        (live_hbm, live_ref),
        (gain_hbm, gain_ref),
        (plants_hbm, plants_ref),
        (inner_hbm, inner_ref),
    )
    words = [
        pltpu.make_async_copy(source, target, word_sem.at[i])
        for i, (source, target) in enumerate(pairs)
    ]
    for load in words + loads:
        load.start()

    barrier = pltpu.get_barrier_semaphore()
    for d in range(1, n_scen):
        pl.semaphore_signal(
            barrier, inc=1, device_id={"scen": lax.rem(scen + d, n_scen)}, device_id_type=MESH
        )
    for d in range(1, n_area):
        pl.semaphore_signal(
            barrier, inc=1, device_id={"area": lax.rem(me + d, n_area)}, device_id_type=MESH
        )

    def to_areas(ref, kind):
        return [
            pltpu.make_async_remote_copy(
                src_ref=ref,
                dst_ref=ref,
                send_sem=send_sem.at[kind, d - 1],
                recv_sem=recv_sem.at[kind, d - 1],
                device_id={"area": lax.rem(me + d, n_area)},
                device_id_type=MESH,
            )
            for d in range(1, n_area)
        ]

    send_prior = to_areas(prior_buf.at[mine], 0)
    send_couple = to_areas(couple_buf.at[mine], 1)
    send_base = to_areas(base_buf.at[mine], 2)
    send_small = to_areas(small_buf.at[my_small], 3)

    def to_scens(ref, target, kind):
        return [
            pltpu.make_async_remote_copy(
                src_ref=ref,
                dst_ref=target.at[d - 1],
                send_sem=scen_send.at[kind, d - 1],
                recv_sem=scen_recv.at[kind, d - 1],
                device_id={"scen": lax.rem(scen + d, n_scen)},
                device_id_type=MESH,
            )
            for d in range(1, n_scen)
        ]

    send_sums = to_scens(sums_buf, sums_in, 0)
    send_edge = to_scens(small_buf, edge_in, 1)

    for word in words:
        word.wait()
    loads[1].wait()
    loads[2].wait()
    pick_row = lax.broadcasted_iota(jnp.int32, (LANES, wide), 0)
    pick_col = lax.broadcasted_iota(jnp.int32, (LANES, wide), 1)
    pick = jnp.where(pick_row - (LANES - BND) == pick_col % BND, 1.0, 0.0).astype(BF16)
    area_of = lax.broadcasted_iota(jnp.int32, (1, wide), 1) // BND
    gain = jnp.zeros((1, wide), F32)
    for j in range(MAXN):
        factor = jnp.where(j < live_ref[0], gain_ref[0, j], 0.0)
        gain = gain + jnp.where(area_of == near_ref[0, j], factor, 0.0)
    couple = (dot(rows_buf[:, order - LANES :], pick) * gain).astype(BF16)
    couple_buf[mine, :] = couple[GEN:]

    place = lax.broadcasted_iota(jnp.int32, (1, order), 1)
    gone = (place >= GEN) & (place < order - BND) & (place - GEN >= inner_ref[0])
    keep = jnp.where(gone, 0.0, 1.0).astype(BF16)
    matrix = rows_buf[...] * keep
    lane = lax.broadcasted_iota(jnp.int32, (1, LANES), 1)
    hour_row = lax.broadcasted_iota(jnp.int32, (hours, LANES), 0)
    hour_col = lax.broadcasted_iota(jnp.int32, (hours, LANES), 1)
    same_hour = jnp.where(hour_row == hour_col % hours, 1.0, 0.0).astype(BF16)
    fold_row = lax.broadcasted_iota(jnp.int32, (LANES, LANES), 0)
    fold_col = lax.broadcasted_iota(jnp.int32, (LANES, LANES), 1)
    fold = jnp.where(fold_row % hours == fold_col % hours, 1.0, 0.0).astype(BF16)
    fold2 = jnp.concatenate([fold, fold], axis=0)
    loads[3].wait()
    level = lax.dot_general(
        matrix, mean_buf[...], (((1,), (1,)), ((), ())), preferred_element_type=F32
    )
    level = dot(halves(level, 1), jnp.concatenate([same_hour, same_hour], axis=0))
    state = jnp.concatenate([level] * (columns // LANES), axis=1)
    for c in range(CHUNKS):
        loads[4 + c].wait()
        state = state + dot(
            matrix[:, c * depth : (c + 1) * depth], spread_buf[pl.ds(c * depth, depth), :]
        )
    base_buf[mine, :] = state[GEN:].astype(BF16)

    scen_of = lax.broadcasted_iota(jnp.int32, (1, columns), 1) // hours
    weight = jnp.zeros((1, columns), F32)
    total = jnp.float32(0.0)
    for s in range(scen_here):
        weight = jnp.where(scen_of == s, raw_ref[s], weight)
        total = total + raw_ref[s]

    loads[0].wait()

    def squeeze(x):
        x = x * weight
        out = x[:, :LANES]
        for k in range(1, columns // LANES):
            out = out + x[:, k * LANES : (k + 1) * LANES]
        return out

    folded = jnp.concatenate([squeeze(state), squeeze(prior_buf[mine, :].astype(F32))], axis=0)
    folded = dot(halves(folded, 1), fold2)
    spot = [jnp.where(lane // hours == k, 1.0, 0.0) for k in range(groups)]

    def pack(x):
        step = x.shape[0] // groups
        out = x[:step] * spot[0]
        for k in range(1, groups):
            out = out + x[k * step : (k + 1) * step] * spot[k]
        return out

    gen_rows = GEN // groups
    sums = jnp.concatenate([pack(folded[:GEN]), jnp.full((8, LANES), total, F32)], axis=0)
    small_buf[my_small, :] = pack(folded[GEN:])
    sums_buf[...] = sums

    pl.semaphore_wait(barrier, n_area + n_scen - 2)
    for copy in send_small + send_sums + send_couple + send_prior + send_base:
        copy.start()
    for copy in send_small:
        copy.wait_recv()
    for copy in send_edge:
        copy.start()

    for copy in send_prior:
        copy.wait_recv()
    for copy in send_couple:
        copy.wait_recv()
    prior = prior_buf[...]
    couples = couple_buf[...]
    first = state[:GEN] + dot(couple[:GEN], prior)
    edge = dot(couples, prior).astype(BF16)
    gen_part = matrix[:, :GEN]
    later = state - penalty * dot(gen_part, first.astype(BF16)) + dot(couple, edge)

    for copy in send_sums:
        copy.wait_recv()
    for d in range(1, n_scen):
        sums = sums + sums_in[d - 1]
    scale = 1.0 / sums[gen_rows:]
    means = sums[:gen_rows] * jnp.concatenate([scale] * (gen_rows // 8), axis=0)
    gen_mean = jnp.concatenate([means[:gen_rows] * spot[k] for k in range(groups)], axis=0)
    gen_mean = dot(halves(gen_mean, 1), fold2)
    for copy in send_edge:
        copy.wait_recv()
    small = small_buf[...]
    for d in range(1, n_scen):
        small = small + edge_in[d - 1]
    small = small * jnp.concatenate([scale] * n_area, axis=0)
    half = groups // 2
    edges = jnp.concatenate(
        [
            small[b * 8 : (b + 1) * 8] * spot[k + first_k]
            for first_k in (0, half)
            for b in range(n_area)
            for k in range(half)
        ],
        axis=0,
    )
    edges = dot(halves(edges, 1), fold2)
    prior_mean = edges[wide:].astype(BF16)
    edge_mean = (edges[:wide] + dot(couples, prior_mean)).astype(BF16)
    mean1 = gen_mean + dot(couple[:GEN], prior_mean)
    slot = lax.broadcasted_iota(jnp.int32, (GEN, LANES), 0)
    alive = jnp.where(slot < plants_ref[0], 1.0, 0.0)
    commit1 = jnp.clip(mean1, 0.0, 1.0) * alive
    both = jnp.concatenate([gen_part, gen_part], axis=1)
    mean2 = (
        gen_mean
        + penalty * dot(both[:GEN], halves(2.0 * commit1 - mean1, 0))
        + dot(couple[:GEN], edge_mean)
    )
    commit2 = jnp.clip(mean2, 0.0, 1.0) * alive
    push = dot(both, halves((2.0 * penalty) * commit1, 0))
    times = columns // LANES
    drop = jnp.concatenate([push[:GEN] - commit1 - commit2] * times, axis=1) + first
    commit_ref[0] = commit2.T[:hours]

    for copy in send_base:
        copy.wait_recv()
    state2 = later + dot(couple, base_buf[...])
    dual_ref[0] = state2[:GEN] + drop
    bound_ref[0] = state2[GEN:] + jnp.concatenate([push[GEN:]] * times, axis=1)

    for copy in send_prior + send_couple + send_base + send_small + send_sums + send_edge:
        copy.wait_send()


def place(*refs):
    count = (len(refs) - 1) // 2
    sems = refs[-1]
    copies = [
        pltpu.make_async_copy(refs[i], refs[count + i], sems.at[i]) for i in range(count)
    ]
    for copy in copies:
        copy.start()
    for copy in copies:
        copy.wait()


def solution(mesh):
    n_area, n_scen = mesh.shape["area"], mesh.shape["scen"]

    def body(matrix, mean, spread, raw, prior, near, live, gain, plants, inner):
        order, columns, hours = matrix.shape[2], spread.shape[2], mean.shape[2]
        hbm = pl.BlockSpec(memory_space=pltpu.HBM)
        vmem = pl.BlockSpec(memory_space=pltpu.VMEM)
        rows = GEN + BND
        wide = n_area * BND
        packed = GEN * hours // LANES + 8
        results = pl.pallas_call(
            functools.partial(kernel, n_area, n_scen),
            out_shape=(
                pltpu.VMEM((1, hours, GEN), F32),
                pltpu.VMEM((1, GEN, columns), F32),
                pltpu.VMEM((1, BND, columns), F32),
            ),
            in_specs=[hbm] * 10,
            out_specs=(vmem,) * 3,
            scratch_shapes=[
                pltpu.SMEM(raw.shape, raw.dtype),
                pltpu.SMEM(near.shape, near.dtype),
                pltpu.SMEM(live.shape, live.dtype),
                pltpu.SMEM(gain.shape, gain.dtype),
                pltpu.SMEM(plants.shape, plants.dtype),
                pltpu.SMEM(inner.shape, inner.dtype),
                pltpu.VMEM((rows, order), BF16),
                pltpu.VMEM((hours, order), BF16),
                pltpu.VMEM((order, columns), BF16),
                pltpu.VMEM((wide, columns), BF16),
                pltpu.VMEM((wide, wide), BF16),
                pltpu.VMEM((wide, columns), BF16),
                pltpu.VMEM((packed, LANES), F32),
                pltpu.VMEM((n_scen - 1, packed, LANES), F32),
                pltpu.VMEM((n_area * 8, LANES), F32),
                pltpu.VMEM((n_scen - 1, n_area * 8, LANES), F32),
                pltpu.SemaphoreType.DMA((4 + CHUNKS,)),
                pltpu.SemaphoreType.DMA((6,)),
                pltpu.SemaphoreType.DMA((4, n_area - 1)),
                pltpu.SemaphoreType.DMA((4, n_area - 1)),
                pltpu.SemaphoreType.DMA((2, n_scen - 1)),
                pltpu.SemaphoreType.DMA((2, n_scen - 1)),
            ],
            compiler_params=pltpu.CompilerParams(
                collective_id=0, has_side_effects=True, vmem_limit_bytes=67043328 - 360 * 2**10
            ),
        )(
            raw,
            near,
            live,
            gain,
            plants,
            inner,
            matrix,
            jnp.swapaxes(mean, 1, 2),
            spread,
            prior,
        )
        commitment, dual, boundary = pl.pallas_call(
            place,
            out_shape=tuple(jax.ShapeDtypeStruct(x.shape, x.dtype) for x in results),
            in_specs=(vmem,) * 3,
            out_specs=(hbm,) * 3,
            scratch_shapes=[pltpu.SemaphoreType.DMA((3,))],
            compiler_params=pltpu.CompilerParams(vmem_limit_bytes=4 * 2**20),
        )(*results)
        return jnp.swapaxes(commitment, 1, 2), dual, boundary

    return jax.shard_map(
        body,
        mesh=mesh,
        in_specs=(
            P(("groups", "area"), None, None),
            P(("groups", "area"), None, None),
            P(("groups", "area"), None, "scen"),
            P(("groups", "scen")),
            P(("groups", "area"), None, "scen"),
            P(("groups", "area"), None),
            P(("groups", "area")),
            P(("groups", "area"), None),
            P(("groups", "area")),
            P(("groups", "area")),
        ),
        out_specs=(
            P(("groups", "area"), None, None),
            P(("groups", "area"), None, "scen"),
            P(("groups", "area"), None, "scen"),
        ),
        check_vma=False,
    )
```

profile of v0, /device:TPU:0, one launch (start us, length us, event | category | flops | bytes accessed | tf_op | source)
XLA Modules:
  0.0 17.4 jit_solution(10205266904308351998)
XLA Ops:
  2.6 14.1 %shard_map.121 = (f32[1,16,128]{2,1,0:T(8,128)S(1)}, f32[1,128,512]{2,1,0:T(8,128)S(1)}, f32[1,32,512]{2,1,0:T(8,128)S(1)}) custom-call(f32[32]{0:T(128)} %raw_hbm.1, s32[1,4]{1,0:T(1,128)} %near_hbm.1, s32[1]{0:T(128)S(6)} %copy.13.live_hbm, f32[1,4]{1,0:T(1,128)} %gain_hbm.1, s32[1]{0:T(128)S(6)} %copy.14.plants_hbm, s32[1]{0:T(128)S(6)} %copy.15.inner_hbm, ...), custom_call_target="tpu_custom_call" | custom-call | tf_op jit(solution)/shard_map/pallas_call | solution.py:324
  16.7 0.7 %shard_map.122 = (f32[1,16,128]{2,1,0:T(8,128)}, f32[1,128,512]{2,1,0:T(8,128)}, f32[1,32,512]{2,1,0:T(8,128)}) custom-call(f32[1,16,128]{2,1,0:T(8,128)S(1)} %get-tuple-element.9.refs_0_, f32[1,128,512]{2,1,0:T(8,128)S(1)} %get-tuple-element.10.refs_1_, f32[1,32,512]{2,1,0:T(8,128)S(1)} %get-tuple-element.11.refs_2_), custom_call_target="tpu_custom_call" | custom-call | tf_op jit(solution)/shard_map/pallas_call | solution.py:372
where the time goes:
time: 17.6 us; the launch traced here: 17.4 us
  Pallas kernels  14.9 us (85%)
  between operations  2.58 us (15%)
    pallas_call x1, Pallas kernels, body(): pl.pallas_call(functools.partial(kernel, n_area, n_scen), out_shape=(pltp...  14.1 us
    pallas_call x1, Pallas kernels, body(): pl.pallas_call(place, out_shape=tuple((jax.ShapeDtypeStruct(x.shape, x.dt...  0.75 us

commit v1 on v0

--- a/solution.py
+++ b/solution.py
@@ -79,6 +79,17 @@
     me = lax.axis_index("area")
     scen = lax.axis_index("scen")
 
+    barrier = pltpu.get_barrier_semaphore()
+    for d in range(1, n_scen):
+        pl.semaphore_signal(
+            barrier, inc=1, device_id={"scen": lax.rem(scen + d, n_scen)}, device_id_type=MESH
+        )
+    for d in range(1, n_area):
+        pl.semaphore_signal(
+            barrier, inc=1, device_id={"area": lax.rem(me + d, n_area)}, device_id_type=MESH
+        )
+
+    others = [k + (k - me + n_area) // n_area for k in range(n_area - 1)]
     mine = pl.ds(pl.multiple_of(me * BND, BND), BND)
     my_small = pl.ds(pl.multiple_of(me * 8, 8), 8)
     loads = [
@@ -111,33 +122,38 @@
     for load in words + loads:
         load.start()
 
-    barrier = pltpu.get_barrier_semaphore()
-    for d in range(1, n_scen):
-        pl.semaphore_signal(
-            barrier, inc=1, device_id={"scen": lax.rem(scen + d, n_scen)}, device_id_type=MESH
-        )
-    for d in range(1, n_area):
-        pl.semaphore_signal(
-            barrier, inc=1, device_id={"area": lax.rem(me + d, n_area)}, device_id_type=MESH
-        )
-
-    def to_areas(ref, kind):
-        return [
+    def to_area(ref, rows_of, kind, area):
+        own = rows_of(me)
+        return pltpu.make_async_remote_copy(
+            src_ref=ref.at[own],
+            dst_ref=ref.at[own],
+            send_sem=send_sem.at[kind, area],
+            recv_sem=recv_sem.at[kind, me],
+            device_id={"area": area},
+            device_id_type=MESH,
+        )
+
+    def arrived(ref, rows_of, kind):
+        for area in others:
+            theirs = ref.at[rows_of(area)]
             pltpu.make_async_remote_copy(
-                src_ref=ref,
-                dst_ref=ref,
-                send_sem=send_sem.at[kind, d - 1],
-                recv_sem=recv_sem.at[kind, d - 1],
-                device_id={"area": lax.rem(me + d, n_area)},
+                src_ref=theirs,
+                dst_ref=theirs,
+                send_sem=send_sem.at[kind, area],
+                recv_sem=recv_sem.at[kind, area],
+                device_id={"area": area},
                 device_id_type=MESH,
-            )
-            for d in range(1, n_area)
-        ]
-
-    send_prior = to_areas(prior_buf.at[mine], 0)
-    send_couple = to_areas(couple_buf.at[mine], 1)
-    send_base = to_areas(base_buf.at[mine], 2)
-    send_small = to_areas(small_buf.at[my_small], 3)
+            ).wait_recv()
+
+    def tie_rows(area):
+        return pl.ds(pl.multiple_of(area * BND, BND), BND)
+
+    def small_rows(area):
+        return pl.ds(pl.multiple_of(area * 8, 8), 8)
+
+    kinds = ((prior_buf, tie_rows), (couple_buf, tie_rows), (base_buf, tie_rows))
+    bulk = [[to_area(*pair, i, a) for i, pair in enumerate(kinds)] for a in others]
+    send_small = [to_area(small_buf, small_rows, 3, a) for a in others]
 
     def to_scens(ref, target, kind):
         return [
@@ -228,17 +244,18 @@
     sums_buf[...] = sums
 
     pl.semaphore_wait(barrier, n_area + n_scen - 2)
-    for copy in send_small + send_sums + send_couple + send_prior + send_base:
+    for copy in send_small + send_sums + bulk[0]:
         copy.start()
-    for copy in send_small:
-        copy.wait_recv()
+    for copy in bulk[0]:
+        copy.wait_send()
+    for copy in sum(bulk[1:], []):
+        copy.start()
+    arrived(small_buf, small_rows, 3)
     for copy in send_edge:
         copy.start()
 
-    for copy in send_prior:
-        copy.wait_recv()
-    for copy in send_couple:
-        copy.wait_recv()
+    arrived(prior_buf, tie_rows, 0)
+    arrived(couple_buf, tie_rows, 1)
     prior = prior_buf[...]
     couples = couple_buf[...]
     first = state[:GEN] + dot(couple[:GEN], prior)
@@ -289,13 +306,12 @@
     drop = jnp.concatenate([push[:GEN] - commit1 - commit2] * times, axis=1) + first
     commit_ref[0] = commit2.T[:hours]
 
-    for copy in send_base:
-        copy.wait_recv()
+    arrived(base_buf, tie_rows, 2)
     state2 = later + dot(couple, base_buf[...])
     dual_ref[0] = state2[:GEN] + drop
     bound_ref[0] = state2[GEN:] + jnp.concatenate([push[GEN:]] * times, axis=1)
 
-    for copy in send_prior + send_couple + send_base + send_small + send_sums + send_edge:
+    for copy in sum(bulk[1:], send_small + send_sums + send_edge):
         copy.wait_send()
 
 
@@ -349,8 +365,8 @@
                 pltpu.VMEM((n_scen - 1, n_area * 8, LANES), F32),
                 pltpu.SemaphoreType.DMA((4 + CHUNKS,)),
                 pltpu.SemaphoreType.DMA((6,)),
-                pltpu.SemaphoreType.DMA((4, n_area - 1)),
-                pltpu.SemaphoreType.DMA((4, n_area - 1)),
+                pltpu.SemaphoreType.DMA((4, n_area)),
+                pltpu.SemaphoreType.DMA((4, n_area)),
                 pltpu.SemaphoreType.DMA((2, n_scen - 1)),
                 pltpu.SemaphoreType.DMA((2, n_scen - 1)),
             ],

time: 17.6 us -> 17.2 us (0.977)
  Pallas kernels: 14.9 us -> 14.5 us
    pallas_call x1, Pallas kernels: 14.1 us -> 13.7 us  [body(): pl.pallas_call(functools.partial(kernel, n_area, n_scen), out_shape=(pltp...]
where the time goes in v1:
time: 17.2 us; the launch traced here: 17.1 us
  Pallas kernels  14.5 us (84%)
  between operations  2.58 us (15%)
    pallas_call x1, Pallas kernels, body(): pl.pallas_call(functools.partial(kernel, n_area, n_scen), out_shape=(pltp...  13.7 us
    pallas_call x1, Pallas kernels, body(): pl.pallas_call(place, out_shape=tuple((jax.ShapeDtypeStruct(x.shape, x.dt...  0.75 us

profile of v1, /device:TPU:0, one launch (start us, length us, event | category | flops | bytes accessed | tf_op | source)
XLA Modules:
  0.0 17.1 jit_solution(8264262673249412297)
XLA Ops:
  2.6 13.7 %shard_map.121 = (f32[1,16,128]{2,1,0:T(8,128)S(1)}, f32[1,128,512]{2,1,0:T(8,128)S(1)}, f32[1,32,512]{2,1,0:T(8,128)S(1)}) custom-call(f32[32]{0:T(128)} %raw_hbm.1, s32[1,4]{1,0:T(1,128)} %near_hbm.1, s32[1]{0:T(128)S(6)} %copy.13.live_hbm, f32[1,4]{1,0:T(1,128)} %gain_hbm.1, s32[1]{0:T(128)S(6)} %copy.14.plants_hbm, s32[1]{0:T(128)S(6)} %copy.15.inner_hbm, ...), custom_call_target="tpu_custom_call" | custom-call | tf_op jit(solution)/shard_map/pallas_call | solution.py:340
  16.3 0.7 %shard_map.122 = (f32[1,16,128]{2,1,0:T(8,128)}, f32[1,128,512]{2,1,0:T(8,128)}, f32[1,32,512]{2,1,0:T(8,128)}) custom-call(f32[1,16,128]{2,1,0:T(8,128)S(1)} %get-tuple-element.9.refs_0_, f32[1,128,512]{2,1,0:T(8,128)S(1)} %get-tuple-element.10.refs_1_, f32[1,32,512]{2,1,0:T(8,128)S(1)} %get-tuple-element.11.refs_2_), custom_call_target="tpu_custom_call" | custom-call | tf_op jit(solution)/shard_map/pallas_call | solution.py:388

commit v2 on v1

--- a/solution.py
+++ b/solution.py
@@ -11,7 +11,7 @@
 BND = 32
 MAXN = 4
 LANES = 128
-CHUNKS = 4
+CHUNKS = 1
 MESH = pl.DeviceIdType.MESH
 F32 = jnp.float32
 BF16 = jnp.bfloat16
@@ -74,39 +74,31 @@
     scen_here = raw_ref.shape[0]
     rows = GEN + BND
     groups = LANES // hours
-    depth = order // CHUNKS
+    width = columns // CHUNKS
     wide = n_area * BND
     me = lax.axis_index("area")
     scen = lax.axis_index("scen")
 
-    barrier = pltpu.get_barrier_semaphore()
-    for d in range(1, n_scen):
-        pl.semaphore_signal(
-            barrier, inc=1, device_id={"scen": lax.rem(scen + d, n_scen)}, device_id_type=MESH
-        )
-    for d in range(1, n_area):
-        pl.semaphore_signal(
-            barrier, inc=1, device_id={"area": lax.rem(me + d, n_area)}, device_id_type=MESH
-        )
-
     others = [k + (k - me + n_area) // n_area for k in range(n_area - 1)]
     mine = pl.ds(pl.multiple_of(me * BND, BND), BND)
     my_small = pl.ds(pl.multiple_of(me * 8, 8), 8)
-    loads = [
-        pltpu.make_async_copy(prior_ref.at[0], prior_buf.at[mine], load_sem.at[0]),
+    rows_in = [
         pltpu.make_async_copy(
-            matrix_ref.at[0, pl.ds(0, GEN)], rows_buf.at[pl.ds(0, GEN)], load_sem.at[1]
+            matrix_ref.at[0, pl.ds(0, GEN)], rows_buf.at[pl.ds(0, GEN)], load_sem.at[0]
         ),
         pltpu.make_async_copy(
-            matrix_ref.at[0, pl.ds(order - BND, BND)], rows_buf.at[pl.ds(GEN, BND)], load_sem.at[2]
+            matrix_ref.at[0, pl.ds(order - BND, BND)], rows_buf.at[pl.ds(GEN, BND)], load_sem.at[1]
         ),
-        pltpu.make_async_copy(mean_ref.at[0], mean_buf, load_sem.at[3]),
     ]
-    for c in range(CHUNKS):
-        part = pl.ds(c * depth, depth)
-        loads.append(
-            pltpu.make_async_copy(spread_ref.at[0, part], spread_buf.at[part], load_sem.at[4 + c])
-        )
+    mean_in = pltpu.make_async_copy(mean_ref.at[0], mean_buf, load_sem.at[2])
+    prior_in = pltpu.make_async_copy(prior_ref.at[0], prior_buf.at[mine], load_sem.at[3])
+    parts = [pl.ds(c * width, width) for c in range(CHUNKS)]
+    spread_in = [
+        pltpu.make_async_copy(
+            spread_ref.at[0, :, part], spread_buf.at[:, part], load_sem.at[4 + c]
+        )
+        for c, part in enumerate(parts)
+    ]
     pairs = (
         (raw_hbm, raw_ref),
         (near_hbm, near_ref),
@@ -119,8 +111,18 @@
         pltpu.make_async_copy(source, target, word_sem.at[i])
         for i, (source, target) in enumerate(pairs)
     ]
-    for load in words + loads:
+    for load in words + rows_in + [mean_in] + spread_in + [prior_in]:
         load.start()
+    barrier = pltpu.get_barrier_semaphore()
+    for d in range(1, n_scen):
+        pl.semaphore_signal(
+            barrier, inc=1, device_id={"scen": lax.rem(scen + d, n_scen)}, device_id_type=MESH
+        )
+    for d in range(1, n_area):
+        pl.semaphore_signal(
+            barrier, inc=1, device_id={"area": lax.rem(me + d, n_area)}, device_id_type=MESH
+        )
+
 
     def to_area(ref, rows_of, kind, area):
         own = rows_of(me)
@@ -173,8 +175,8 @@
 
     for word in words:
         word.wait()
-    loads[1].wait()
-    loads[2].wait()
+    for load in rows_in:
+        load.wait()
     pick_row = lax.broadcasted_iota(jnp.int32, (LANES, wide), 0)
     pick_col = lax.broadcasted_iota(jnp.int32, (LANES, wide), 1)
     pick = jnp.where(pick_row - (LANES - BND) == pick_col % BND, 1.0, 0.0).astype(BF16)
@@ -198,17 +200,18 @@
     fold_col = lax.broadcasted_iota(jnp.int32, (LANES, LANES), 1)
     fold = jnp.where(fold_row % hours == fold_col % hours, 1.0, 0.0).astype(BF16)
     fold2 = jnp.concatenate([fold, fold], axis=0)
-    loads[3].wait()
+    mean_in.wait()
     level = lax.dot_general(
         matrix, mean_buf[...], (((1,), (1,)), ((), ())), preferred_element_type=F32
     )
     level = dot(halves(level, 1), jnp.concatenate([same_hour, same_hour], axis=0))
-    state = jnp.concatenate([level] * (columns // LANES), axis=1)
-    for c in range(CHUNKS):
-        loads[4 + c].wait()
-        state = state + dot(
-            matrix[:, c * depth : (c + 1) * depth], spread_buf[pl.ds(c * depth, depth), :]
-        )
+    states = []
+    for load, part in zip(spread_in, parts):
+        load.wait()
+        states.append(
+            dot(matrix, spread_buf[:, part]) + jnp.concatenate([level] * (width // LANES), axis=1)
+        )
+    state = jnp.concatenate(states, axis=1)
     base_buf[mine, :] = state[GEN:].astype(BF16)
 
     scen_of = lax.broadcasted_iota(jnp.int32, (1, columns), 1) // hours
@@ -218,7 +221,7 @@
         weight = jnp.where(scen_of == s, raw_ref[s], weight)
         total = total + raw_ref[s]
 
-    loads[0].wait()
+    prior_in.wait()
 
     def squeeze(x):
         x = x * weight
@@ -246,7 +249,7 @@
     pl.semaphore_wait(barrier, n_area + n_scen - 2)
     for copy in send_small + send_sums + bulk[0]:
         copy.start()
-    for copy in bulk[0]:
+    for copy in bulk[0][:2]:
         copy.wait_send()
     for copy in sum(bulk[1:], []):
         copy.start()
@@ -311,7 +314,7 @@
     dual_ref[0] = state2[:GEN] + drop
     bound_ref[0] = state2[GEN:] + jnp.concatenate([push[GEN:]] * times, axis=1)
 
-    for copy in sum(bulk[1:], send_small + send_sums + send_edge):
+    for copy in sum(bulk[1:], send_small + send_sums + send_edge + bulk[0][2:]):
         copy.wait_send()
 
 

time: 17.2 us -> 16.9 us (0.983)
  Pallas kernels: 14.5 us -> 14.1 us
    pallas_call x1, Pallas kernels: 13.7 us -> 13.4 us  [body(): pl.pallas_call(functools.partial(kernel, n_area, n_scen), out_shape=(pltp...]
where the time goes in v2:
time: 16.9 us; the launch traced here: 16.7 us
  Pallas kernels  14.1 us (83%)
  between operations  2.58 us (15%)
    pallas_call x1, Pallas kernels, body(): pl.pallas_call(functools.partial(kernel, n_area, n_scen), out_shape=(pltp...  13.4 us
    pallas_call x1, Pallas kernels, body(): pl.pallas_call(place, out_shape=tuple((jax.ShapeDtypeStruct(x.shape, x.dt...  0.75 us

profile of v2, /device:TPU:0, one launch (start us, length us, event | category | flops | bytes accessed | tf_op | source)
XLA Modules:
  0.0 16.7 jit_solution(9915897202973848903)
XLA Ops:
  2.6 13.4 %shard_map.121 = (f32[1,16,128]{2,1,0:T(8,128)S(1)}, f32[1,128,512]{2,1,0:T(8,128)S(1)}, f32[1,32,512]{2,1,0:T(8,128)S(1)}) custom-call(f32[32]{0:T(128)} %raw_hbm.1, s32[1,4]{1,0:T(1,128)} %near_hbm.1, s32[1]{0:T(128)S(6)} %copy.13.live_hbm, f32[1,4]{1,0:T(1,128)} %gain_hbm.1, s32[1]{0:T(128)S(6)} %copy.14.plants_hbm, s32[1]{0:T(128)S(6)} %copy.15.inner_hbm, ...), custom_call_target="tpu_custom_call" | custom-call | tf_op jit(solution)/shard_map/pallas_call | solution.py:343
  15.9 0.7 %shard_map.122 = (f32[1,16,128]{2,1,0:T(8,128)}, f32[1,128,512]{2,1,0:T(8,128)}, f32[1,32,512]{2,1,0:T(8,128)}) custom-call(f32[1,16,128]{2,1,0:T(8,128)S(1)} %get-tuple-element.9.refs_0_, f32[1,128,512]{2,1,0:T(8,128)S(1)} %get-tuple-element.10.refs_1_, f32[1,32,512]{2,1,0:T(8,128)S(1)} %get-tuple-element.11.refs_2_), custom_call_target="tpu_custom_call" | custom-call | tf_op jit(solution)/shard_map/pallas_call | solution.py:391

commit v3 on v2

--- a/solution.py
+++ b/solution.py
@@ -12,6 +12,7 @@
 MAXN = 4
 LANES = 128
 CHUNKS = 1
+EARLY = 2
 MESH = pl.DeviceIdType.MESH
 F32 = jnp.float32
 BF16 = jnp.bfloat16
@@ -61,12 +62,17 @@
     sums_in,
     small_buf,
     edge_in,
+    direct_buf,
+    total_buf,
     load_sem,
     word_sem,
     send_sem,
     recv_sem,
     scen_send,
     scen_recv,
+    direct_send,
+    direct_recv,
+    turn_sem,
 ):
     order = matrix_ref.shape[2]
     columns = spread_ref.shape[2]
@@ -81,7 +87,6 @@
 
     others = [k + (k - me + n_area) // n_area for k in range(n_area - 1)]
     mine = pl.ds(pl.multiple_of(me * BND, BND), BND)
-    my_small = pl.ds(pl.multiple_of(me * 8, 8), 8)
     rows_in = [
         pltpu.make_async_copy(
             matrix_ref.at[0, pl.ds(0, GEN)], rows_buf.at[pl.ds(0, GEN)], load_sem.at[0]
@@ -111,9 +116,18 @@
         pltpu.make_async_copy(source, target, word_sem.at[i])
         for i, (source, target) in enumerate(pairs)
     ]
-    for load in words + rows_in + [mean_in] + spread_in + [prior_in]:
+    for load in words + rows_in + [mean_in, prior_in] + spread_in:
         load.start()
     barrier = pltpu.get_barrier_semaphore()
+    lead = (me == 0) & (scen < EARLY)
+
+    @pl.when(lead)
+    def _():
+        for area in others:
+            for d in range(1, n_scen):
+                peer = {"area": area, "scen": lax.rem(scen + d, n_scen)}
+                pl.semaphore_signal(barrier, inc=1, device_id=peer, device_id_type=MESH)
+
     for d in range(1, n_scen):
         pl.semaphore_signal(
             barrier, inc=1, device_id={"scen": lax.rem(scen + d, n_scen)}, device_id_type=MESH
@@ -151,7 +165,7 @@
         return pl.ds(pl.multiple_of(area * BND, BND), BND)
 
     def small_rows(area):
-        return pl.ds(pl.multiple_of(area * 8, 8), 8)
+        return area
 
     kinds = ((prior_buf, tie_rows), (couple_buf, tie_rows), (base_buf, tie_rows))
     bulk = [[to_area(*pair, i, a) for i, pair in enumerate(kinds)] for a in others]
@@ -172,6 +186,33 @@
 
     send_sums = to_scens(sums_buf, sums_in, 0)
     send_edge = to_scens(small_buf, edge_in, 1)
+    turns = [lax.rem(scen + d, n_scen) for d in range(n_scen)]
+
+    def direct(target, area, source):
+        return pltpu.make_async_remote_copy(
+            src_ref=small_buf.at[me],
+            dst_ref=direct_buf.at[area * n_scen + source],
+            send_sem=direct_send.at[target],
+            recv_sem=direct_recv.at[area * n_scen + source],
+            device_id={"area": 0, "scen": target},
+            device_id_type=MESH,
+        )
+
+    def send_direct(act):
+        for target in range(EARLY):
+            copy = direct(target, me, scen)
+
+            @pl.when(scen != target)
+            def _():
+                act(copy)
+
+    def send_edges(act):
+        for d in range(1, n_scen):
+
+            @pl.when((me > 0) | (turns[d] >= EARLY))
+            def _():
+                act(send_edge[d - 1])
+
 
     for word in words:
         word.wait()
@@ -205,15 +246,6 @@
         matrix, mean_buf[...], (((1,), (1,)), ((), ())), preferred_element_type=F32
     )
     level = dot(halves(level, 1), jnp.concatenate([same_hour, same_hour], axis=0))
-    states = []
-    for load, part in zip(spread_in, parts):
-        load.wait()
-        states.append(
-            dot(matrix, spread_buf[:, part]) + jnp.concatenate([level] * (width // LANES), axis=1)
-        )
-    state = jnp.concatenate(states, axis=1)
-    base_buf[mine, :] = state[GEN:].astype(BF16)
-
     scen_of = lax.broadcasted_iota(jnp.int32, (1, columns), 1) // hours
     weight = jnp.zeros((1, columns), F32)
     total = jnp.float32(0.0)
@@ -221,8 +253,6 @@
         weight = jnp.where(scen_of == s, raw_ref[s], weight)
         total = total + raw_ref[s]
 
-    prior_in.wait()
-
     def squeeze(x):
         x = x * weight
         out = x[:, :LANES]
@@ -230,10 +260,6 @@
             out = out + x[:, k * LANES : (k + 1) * LANES]
         return out
 
-    folded = jnp.concatenate([squeeze(state), squeeze(prior_buf[mine, :].astype(F32))], axis=0)
-    folded = dot(halves(folded, 1), fold2)
-    spot = [jnp.where(lane // hours == k, 1.0, 0.0) for k in range(groups)]
-
     def pack(x):
         step = x.shape[0] // groups
         out = x[:step] * spot[0]
@@ -241,21 +267,75 @@
             out = out + x[k * step : (k + 1) * step] * spot[k]
         return out
 
+    prior_in.wait()
+    old = squeeze(prior_buf[mine, :].astype(F32))
+    states = []
+    for load, part in zip(spread_in, parts):
+        load.wait()
+        states.append(
+            dot(matrix, spread_buf[:, part]) + jnp.concatenate([level] * (width // LANES), axis=1)
+        )
+    state = jnp.concatenate(states, axis=1)
+
+    base_buf[mine, :] = state[GEN:].astype(BF16)
+    far = (me + n_area - 1) // n_area
+    late = (scen + n_scen - EARLY) // n_scen
+    pl.semaphore_wait(barrier, n_area + n_scen - 2 + far * (EARLY - 1 + late))
+    for some in bulk:
+        some[1].start()
+    spot = [jnp.where(lane // hours == k, 1.0, 0.0) for k in range(groups)]
+    folded = jnp.concatenate([squeeze(state[GEN:]), old], axis=0)
+    small_buf[me] = pack(dot(halves(folded, 1), fold2)).astype(BF16)
+
+    send_direct(lambda copy: copy.start())
+    for copy in send_small:
+        copy.start()
+
     gen_rows = GEN // groups
-    sums = jnp.concatenate([pack(folded[:GEN]), jnp.full((8, LANES), total, F32)], axis=0)
-    small_buf[my_small, :] = pack(folded[GEN:])
+    folded = dot(halves(squeeze(state[:GEN]), 1), fold2)
+    sums = jnp.concatenate([pack(folded), jnp.full((8, LANES), total, F32)], axis=0)
     sums_buf[...] = sums
-
-    pl.semaphore_wait(barrier, n_area + n_scen - 2)
-    for copy in send_small + send_sums + bulk[0]:
+    for copy in send_sums:
         copy.start()
+    odd = (me > 0) & (scen == 1)
+    even = (me > 0) & (scen == 0)
+    bulk[0][0].start()
+
+    @pl.when(odd)
+    def _():
+        pl.semaphore_wait(turn_sem, 1)
+
+    bulk[0][2].start()
+    for k in range(1, n_area - 1):
+
+        @pl.when(k >= me)
+        def _():
+            for copy in bulk[k][::2]:
+                copy.start()
+
+    for k in range(1, n_area - 1):
+
+        @pl.when(k < me)
+        def _():
+            bulk[k][0].start()
+
     for copy in bulk[0][:2]:
         copy.wait_send()
-    for copy in sum(bulk[1:], []):
-        copy.start()
+
+    @pl.when(even)
+    def _():
+        pl.semaphore_signal(
+            turn_sem, inc=1, device_id={"scen": scen + 1}, device_id_type=MESH
+        )
+
+    for k in range(1, n_area - 1):
+
+        @pl.when(k < me)
+        def _():
+            bulk[k][2].start()
+
     arrived(small_buf, small_rows, 3)
-    for copy in send_edge:
-        copy.start()
+    send_edges(lambda copy: copy.start())
 
     arrived(prior_buf, tie_rows, 0)
     arrived(couple_buf, tie_rows, 1)
@@ -274,11 +354,24 @@
     means = sums[:gen_rows] * jnp.concatenate([scale] * (gen_rows // 8), axis=0)
     gen_mean = jnp.concatenate([means[:gen_rows] * spot[k] for k in range(groups)], axis=0)
     gen_mean = dot(halves(gen_mean, 1), fold2)
-    for copy in send_edge:
-        copy.wait_recv()
-    small = small_buf[...]
-    for d in range(1, n_scen):
-        small = small + edge_in[d - 1]
+    total_buf[...] = small_buf[...].astype(F32).reshape(total_buf.shape)
+
+    @pl.when(lead)
+    def _():
+        for area in range(n_area):
+            rows_of = slice(area * 8, (area + 1) * 8)
+            for d in range(1, n_scen):
+                direct(0, area, turns[d]).wait_recv()
+                total_buf[rows_of] += direct_buf[area * n_scen + turns[d]].astype(F32)
+
+    @pl.when(jnp.logical_not(lead))
+    def _():
+        for copy in send_edge:
+            copy.wait_recv()
+        for d in range(1, n_scen):
+            total_buf[...] += edge_in[d - 1].astype(F32).reshape(total_buf.shape)
+
+    small = total_buf[...]
     small = small * jnp.concatenate([scale] * n_area, axis=0)
     half = groups // 2
     edges = jnp.concatenate(
@@ -314,8 +407,10 @@
     dual_ref[0] = state2[:GEN] + drop
     bound_ref[0] = state2[GEN:] + jnp.concatenate([push[GEN:]] * times, axis=1)
 
-    for copy in sum(bulk[1:], send_small + send_sums + send_edge + bulk[0][2:]):
+    for copy in sum(bulk[1:], send_small + send_sums + bulk[0][2:]):
         copy.wait_send()
+    send_direct(lambda copy: copy.wait_send())
+    send_edges(lambda copy: copy.wait_send())
 
 
 def place(*refs):
@@ -364,14 +459,19 @@
                 pltpu.VMEM((wide, columns), BF16),
                 pltpu.VMEM((packed, LANES), F32),
                 pltpu.VMEM((n_scen - 1, packed, LANES), F32),
+                pltpu.VMEM((n_area, 8, LANES), BF16),
+                pltpu.VMEM((n_scen - 1, n_area, 8, LANES), BF16),
+                pltpu.VMEM((n_area * n_scen, 8, LANES), BF16),
                 pltpu.VMEM((n_area * 8, LANES), F32),
-                pltpu.VMEM((n_scen - 1, n_area * 8, LANES), F32),
                 pltpu.SemaphoreType.DMA((4 + CHUNKS,)),
                 pltpu.SemaphoreType.DMA((6,)),
                 pltpu.SemaphoreType.DMA((4, n_area)),
                 pltpu.SemaphoreType.DMA((4, n_area)),
                 pltpu.SemaphoreType.DMA((2, n_scen - 1)),
                 pltpu.SemaphoreType.DMA((2, n_scen - 1)),
+                pltpu.SemaphoreType.DMA((EARLY,)),
+                pltpu.SemaphoreType.DMA((n_area * n_scen,)),
+                pltpu.SemaphoreType.REGULAR,
             ],
             compiler_params=pltpu.CompilerParams(
                 collective_id=0, has_side_effects=True, vmem_limit_bytes=67043328 - 360 * 2**10

time: 16.9 us -> 16.2 us (0.959)
  Pallas kernels: 14.1 us -> 13.4 us
    pallas_call x1, Pallas kernels: 13.4 us -> 12.7 us  [body(): pl.pallas_call(functools.partial(kernel, n_area, n_scen), out_shape=(pltp...]
where the time goes in v3:
time: 16.2 us; the launch traced here: 16 us
  Pallas kernels  13.4 us (83%)
  between operations  2.58 us (16%)
    pallas_call x1, Pallas kernels, body(): pl.pallas_call(functools.partial(kernel, n_area, n_scen), out_shape=(pltp...  12.7 us
    pallas_call x1, Pallas kernels, body(): pl.pallas_call(place, out_shape=tuple((jax.ShapeDtypeStruct(x.shape, x.dt...  0.75 us

profile of v3, /device:TPU:0, one launch (start us, length us, event | category | flops | bytes accessed | tf_op | source)
XLA Modules:
  0.0 16.0 jit_solution(16238582170800597760)
XLA Ops:
  2.6 12.7 %shard_map.121 = (f32[1,16,128]{2,1,0:T(8,128)S(1)}, f32[1,128,512]{2,1,0:T(8,128)S(1)}, f32[1,32,512]{2,1,0:T(8,128)S(1)}) custom-call(f32[32]{0:T(128)} %raw_hbm.1, s32[1,4]{1,0:T(1,128)} %near_hbm.1, s32[1]{0:T(128)S(6)} %copy.13.live_hbm, f32[1,4]{1,0:T(1,128)} %gain_hbm.1, s32[1]{0:T(128)S(6)} %copy.14.plants_hbm, s32[1]{0:T(128)S(6)} %copy.15.inner_hbm, ...), custom_call_target="tpu_custom_call" | custom-call | tf_op jit(solution)/shard_map/pallas_call | solution.py:438
  15.3 0.7 %shard_map.122 = (f32[1,16,128]{2,1,0:T(8,128)}, f32[1,128,512]{2,1,0:T(8,128)}, f32[1,32,512]{2,1,0:T(8,128)}) custom-call(f32[1,16,128]{2,1,0:T(8,128)S(1)} %get-tuple-element.9.refs_0_, f32[1,128,512]{2,1,0:T(8,128)S(1)} %get-tuple-element.10.refs_1_, f32[1,32,512]{2,1,0:T(8,128)S(1)} %get-tuple-element.11.refs_2_), custom_call_target="tpu_custom_call" | custom-call | tf_op jit(solution)/shard_map/pallas_call | solution.py:491

commit v4 on v3

--- a/solution.py
+++ b/solution.py
@@ -167,7 +167,7 @@
     def small_rows(area):
         return area
 
-    kinds = ((prior_buf, tie_rows), (couple_buf, tie_rows), (base_buf, tie_rows))
+    kinds = ((prior_buf, tie_rows), (couple_buf, small_rows), (base_buf, tie_rows))
     bulk = [[to_area(*pair, i, a) for i, pair in enumerate(kinds)] for a in others]
     send_small = [to_area(small_buf, small_rows, 3, a) for a in others]
 
@@ -226,8 +226,16 @@
     for j in range(MAXN):
         factor = jnp.where(j < live_ref[0], gain_ref[0, j], 0.0)
         gain = gain + jnp.where(area_of == near_ref[0, j], factor, 0.0)
-    couple = (dot(rows_buf[:, order - LANES :], pick) * gain).astype(BF16)
-    couple_buf[mine, :] = couple[GEN:]
+    corner = dot(rows_buf[:, order - LANES :], pick)
+    couple = (corner * gain).astype(BF16)
+    eights = BND // 8
+    high = gain.astype(BF16).astype(F32)
+    part_row = lax.broadcasted_iota(jnp.int32, (8, wide), 0)
+    thin = jnp.zeros((8, wide), F32)
+    for q in range(eights):
+        thin = thin + jnp.where(area_of == q, corner[GEN + q * 8 : GEN + q * 8 + 8], 0.0)
+    gains = jnp.where(part_row < 4, high, gain - high)
+    couple_buf[me] = jnp.concatenate([thin, gains], axis=0).astype(BF16)
 
     place = lax.broadcasted_iota(jnp.int32, (1, order), 1)
     gone = (place >= GEN) & (place < order - BND) & (place - GEN >= inner_ref[0])
@@ -301,11 +309,10 @@
     even = (me > 0) & (scen == 0)
     bulk[0][0].start()
 
-    @pl.when(odd)
+    @pl.when(jnp.logical_not(odd))
     def _():
-        pl.semaphore_wait(turn_sem, 1)
-
-    bulk[0][2].start()
+        bulk[0][2].start()
+
     for k in range(1, n_area - 1):
 
         @pl.when(k >= me)
@@ -319,6 +326,11 @@
         def _():
             bulk[k][0].start()
 
+    @pl.when(odd)
+    def _():
+        pl.semaphore_wait(turn_sem, 1)
+        bulk[0][2].start()
+
     for copy in bulk[0][:2]:
         copy.wait_send()
 
@@ -338,9 +350,20 @@
     send_edges(lambda copy: copy.start())
 
     arrived(prior_buf, tie_rows, 0)
-    arrived(couple_buf, tie_rows, 1)
+    arrived(couple_buf, small_rows, 1)
     prior = prior_buf[...]
-    couples = couple_buf[...]
+    thin = couple_buf[...].astype(F32)
+    slots = [jnp.where(lane // BND == q, 1.0, 0.0) for q in range(eights)]
+    couples = jnp.concatenate(
+        [thin[b, :8, :LANES] * slots[q] for b in range(n_area) for q in range(eights)], axis=0
+    )
+    tie_row = lax.broadcasted_iota(jnp.int32, (LANES, wide), 0)
+    same_tie = jnp.where(tie_row % BND == pick_col % BND, 1.0, 0.0).astype(BF16)
+    gains = jnp.concatenate(
+        [jnp.broadcast_to(thin[b, 8:9] + thin[b, 12:13], (BND, wide)) for b in range(n_area)],
+        axis=0,
+    )
+    couples = (dot(couples.astype(BF16), same_tie) * gains).astype(BF16)
     first = state[:GEN] + dot(couple[:GEN], prior)
     edge = dot(couples, prior).astype(BF16)
     gen_part = matrix[:, :GEN]
@@ -455,7 +478,7 @@
                 pltpu.VMEM((hours, order), BF16),
                 pltpu.VMEM((order, columns), BF16),
                 pltpu.VMEM((wide, columns), BF16),
-                pltpu.VMEM((wide, wide), BF16),
+                pltpu.VMEM((n_area, 16, wide), BF16),
                 pltpu.VMEM((wide, columns), BF16),
                 pltpu.VMEM((packed, LANES), F32),
                 pltpu.VMEM((n_scen - 1, packed, LANES), F32),

time: 16.2 us -> 16.1 us (level)
  no operation moved by 1% of the time
where the time goes in v4:
time: 16.1 us; the launch traced here: 15.9 us
  Pallas kernels  13.3 us (83%)
  between operations  2.58 us (16%)
    pallas_call x1, Pallas kernels, body(): pl.pallas_call(functools.partial(kernel, n_area, n_scen), out_shape=(pltp...  12.5 us
    pallas_call x1, Pallas kernels, body(): pl.pallas_call(place, out_shape=tuple((jax.ShapeDtypeStruct(x.shape, x.dt...  0.75 us

profile of v4, /device:TPU:0, one launch (start us, length us, event | category | flops | bytes accessed | tf_op | source)
XLA Modules:
  0.0 15.9 jit_solution(17443010517026950192)
XLA Ops:
  2.6 12.5 %shard_map.121 = (f32[1,16,128]{2,1,0:T(8,128)S(1)}, f32[1,128,512]{2,1,0:T(8,128)S(1)}, f32[1,32,512]{2,1,0:T(8,128)S(1)}) custom-call(f32[32]{0:T(128)} %raw_hbm.1, s32[1,4]{1,0:T(1,128)} %near_hbm.1, s32[1]{0:T(128)S(6)} %copy.13.live_hbm, f32[1,4]{1,0:T(1,128)} %gain_hbm.1, s32[1]{0:T(128)S(6)} %copy.14.plants_hbm, s32[1]{0:T(128)S(6)} %copy.15.inner_hbm, ...), custom_call_target="tpu_custom_call" | custom-call | tf_op jit(solution)/shard_map/pallas_call | solution.py:461
  15.1 0.7 %shard_map.122 = (f32[1,16,128]{2,1,0:T(8,128)}, f32[1,128,512]{2,1,0:T(8,128)}, f32[1,32,512]{2,1,0:T(8,128)}) custom-call(f32[1,16,128]{2,1,0:T(8,128)S(1)} %get-tuple-element.9.refs_0_, f32[1,128,512]{2,1,0:T(8,128)S(1)} %get-tuple-element.10.refs_1_, f32[1,32,512]{2,1,0:T(8,128)S(1)} %get-tuple-element.11.refs_2_), custom_call_target="tpu_custom_call" | custom-call | tf_op jit(solution)/shard_map/pallas_call | solution.py:514

commit v5 on v4

--- a/solution.py
+++ b/solution.py
@@ -116,7 +116,7 @@
         pltpu.make_async_copy(source, target, word_sem.at[i])
         for i, (source, target) in enumerate(pairs)
     ]
-    for load in words + rows_in + [mean_in, prior_in] + spread_in:
+    for load in [mean_in] + words + rows_in + [prior_in] + spread_in:
         load.start()
     barrier = pltpu.get_barrier_semaphore()
     lead = (me == 0) & (scen < EARLY)
@@ -128,15 +128,15 @@
                 peer = {"area": area, "scen": lax.rem(scen + d, n_scen)}
                 pl.semaphore_signal(barrier, inc=1, device_id=peer, device_id_type=MESH)
 
+
+    for d in range(1, n_area):
+        pl.semaphore_signal(
+            barrier, inc=1, device_id={"area": lax.rem(me + d, n_area)}, device_id_type=MESH
+        )
     for d in range(1, n_scen):
         pl.semaphore_signal(
             barrier, inc=1, device_id={"scen": lax.rem(scen + d, n_scen)}, device_id_type=MESH
         )
-    for d in range(1, n_area):
-        pl.semaphore_signal(
-            barrier, inc=1, device_id={"area": lax.rem(me + d, n_area)}, device_id_type=MESH
-        )
-
 
     def to_area(ref, rows_of, kind, area):
         own = rows_of(me)
@@ -285,7 +285,6 @@
         )
     state = jnp.concatenate(states, axis=1)
 
-    base_buf[mine, :] = state[GEN:].astype(BF16)
     far = (me + n_area - 1) // n_area
     late = (scen + n_scen - EARLY) // n_scen
     pl.semaphore_wait(barrier, n_area + n_scen - 2 + far * (EARLY - 1 + late))
@@ -299,6 +298,8 @@
     for copy in send_small:
         copy.start()
 
+    base_buf[mine, :] = state[GEN:].astype(BF16)
+
     gen_rows = GEN // groups
     folded = dot(halves(squeeze(state[:GEN]), 1), fold2)
     sums = jnp.concatenate([pack(folded), jnp.full((8, LANES), total, F32)], axis=0)
@@ -307,6 +308,7 @@
         copy.start()
     odd = (me > 0) & (scen == 1)
     even = (me > 0) & (scen == 0)
+    held = (me == n_area - 1) & (scen < EARLY)
     bulk[0][0].start()
 
     @pl.when(jnp.logical_not(odd))
@@ -322,7 +324,7 @@
 
     for k in range(1, n_area - 1):
 
-        @pl.when(k < me)
+        @pl.when((k < me) & jnp.logical_not(held))
         def _():
             bulk[k][0].start()
 
@@ -341,6 +343,10 @@
         )
 
     for k in range(1, n_area - 1):
+
+        @pl.when((k < me) & held)
+        def _():
+            bulk[k][0].start()
 
         @pl.when(k < me)
         def _():

time: 16.1 us -> 15.8 us (0.981)
  the two profiles are of different devices: /device:TPU:0 before, /device:TPU:10 now
where the time goes in v5:
time: 15.8 us; the launch traced here: 15.6 us
  Pallas kernels  13.1 us (83%)
  between operations  2.58 us (16%)
    pallas_call x1, Pallas kernels, body(): pl.pallas_call(functools.partial(kernel, n_area, n_scen), out_shape=(pltp...  12.3 us
    pallas_call x1, Pallas kernels, body(): pl.pallas_call(place, out_shape=tuple((jax.ShapeDtypeStruct(x.shape, x.dt...  0.75 us

profile of v5, /device:TPU:10, one launch (start us, length us, event | category | flops | bytes accessed | tf_op | source)
XLA Modules:
  0.0 15.6 jit_solution(3021741423848511656)
XLA Ops:
  2.6 12.3 %shard_map.121 = (f32[1,16,128]{2,1,0:T(8,128)S(1)}, f32[1,128,512]{2,1,0:T(8,128)S(1)}, f32[1,32,512]{2,1,0:T(8,128)S(1)}) custom-call(f32[32]{0:T(128)} %raw_hbm.1, s32[1,4]{1,0:T(1,128)} %near_hbm.1, s32[1]{0:T(128)S(6)} %copy.13.live_hbm, f32[1,4]{1,0:T(1,128)} %gain_hbm.1, s32[1]{0:T(128)S(6)} %copy.14.plants_hbm, s32[1]{0:T(128)S(6)} %copy.15.inner_hbm, ...), custom_call_target="tpu_custom_call" | custom-call | tf_op jit(solution)/shard_map/pallas_call | solution.py:467
  14.9 0.7 %shard_map.122 = (f32[1,16,128]{2,1,0:T(8,128)}, f32[1,128,512]{2,1,0:T(8,128)}, f32[1,32,512]{2,1,0:T(8,128)}) custom-call(f32[1,16,128]{2,1,0:T(8,128)S(1)} %get-tuple-element.9.refs_0_, f32[1,128,512]{2,1,0:T(8,128)S(1)} %get-tuple-element.10.refs_1_, f32[1,32,512]{2,1,0:T(8,128)S(1)} %get-tuple-element.11.refs_2_), custom_call_target="tpu_custom_call" | custom-call | tf_op jit(solution)/shard_map/pallas_call | solution.py:520

commit v6 on v5

--- a/solution.py
+++ b/solution.py
@@ -292,7 +292,7 @@
         some[1].start()
     spot = [jnp.where(lane // hours == k, 1.0, 0.0) for k in range(groups)]
     folded = jnp.concatenate([squeeze(state[GEN:]), old], axis=0)
-    small_buf[me] = pack(dot(halves(folded, 1), fold2)).astype(BF16)
+    small_buf[me] = pack(dot(folded.astype(BF16), fold)).astype(BF16)
 
     send_direct(lambda copy: copy.start())
     for copy in send_small:
@@ -412,7 +412,7 @@
         ],
         axis=0,
     )
-    edges = dot(halves(edges, 1), fold2)
+    edges = dot(edges.astype(BF16), fold)
     prior_mean = edges[wide:].astype(BF16)
     edge_mean = (edges[:wide] + dot(couples, prior_mean)).astype(BF16)
     mean1 = gen_mean + dot(couple[:GEN], prior_mean)

time: 15.8 us -> 15.8 us (level)
  the two profiles are of different devices: /device:TPU:10 before, /device:TPU:14 now
where the time goes in v6:
time: 15.8 us; the launch traced here: 15.6 us
  Pallas kernels  13 us (82%)
  between operations  2.58 us (16%)
    pallas_call x1, Pallas kernels, body(): pl.pallas_call(functools.partial(kernel, n_area, n_scen), out_shape=(pltp...  12.3 us
    pallas_call x1, Pallas kernels, body(): pl.pallas_call(place, out_shape=tuple((jax.ShapeDtypeStruct(x.shape, x.dt...  0.75 us

profile of v6, /device:TPU:14, one launch (start us, length us, event | category | flops | bytes accessed | tf_op | source)
XLA Modules:
  0.0 15.6 jit_solution(16108193687037014462)
XLA Ops:
  2.6 12.3 %shard_map.121 = (f32[1,16,128]{2,1,0:T(8,128)S(1)}, f32[1,128,512]{2,1,0:T(8,128)S(1)}, f32[1,32,512]{2,1,0:T(8,128)S(1)}) custom-call(f32[32]{0:T(128)} %raw_hbm.1, s32[1,4]{1,0:T(1,128)} %near_hbm.1, s32[1]{0:T(128)S(6)} %copy.13.live_hbm, f32[1,4]{1,0:T(1,128)} %gain_hbm.1, s32[1]{0:T(128)S(6)} %copy.14.plants_hbm, s32[1]{0:T(128)S(6)} %copy.15.inner_hbm, ...), custom_call_target="tpu_custom_call" | custom-call | tf_op jit(solution)/shard_map/pallas_call | solution.py:467
  14.8 0.7 %shard_map.122 = (f32[1,16,128]{2,1,0:T(8,128)}, f32[1,128,512]{2,1,0:T(8,128)}, f32[1,32,512]{2,1,0:T(8,128)}) custom-call(f32[1,16,128]{2,1,0:T(8,128)S(1)} %get-tuple-element.9.refs_0_, f32[1,128,512]{2,1,0:T(8,128)S(1)} %get-tuple-element.10.refs_1_, f32[1,32,512]{2,1,0:T(8,128)S(1)} %get-tuple-element.11.refs_2_), custom_call_target="tpu_custom_call" | custom-call | tf_op jit(solution)/shard_map/pallas_call | solution.py:520

commit v7 on v6

--- a/solution.py
+++ b/solution.py
@@ -300,33 +300,34 @@
 
     base_buf[mine, :] = state[GEN:].astype(BF16)
 
+    odd = (me > 0) & (scen == 1)
+    even = (me > 0) & (scen == 0)
+    held = (me == n_area - 1) & (scen < EARLY)
+    bulk[0][0].start()
+
+    @pl.when(jnp.logical_not(odd))
+    def _():
+        bulk[0][2].start()
+
+    for k in range(1, n_area - 1):
+
+        @pl.when(k >= me)
+        def _():
+            for copy in bulk[k][::2]:
+                copy.start()
+
+    for k in range(1, n_area - 1):
+
+        @pl.when((k < me) & jnp.logical_not(held))
+        def _():
+            bulk[k][0].start()
+
     gen_rows = GEN // groups
     folded = dot(halves(squeeze(state[:GEN]), 1), fold2)
     sums = jnp.concatenate([pack(folded), jnp.full((8, LANES), total, F32)], axis=0)
     sums_buf[...] = sums
     for copy in send_sums:
         copy.start()
-    odd = (me > 0) & (scen == 1)
-    even = (me > 0) & (scen == 0)
-    held = (me == n_area - 1) & (scen < EARLY)
-    bulk[0][0].start()
-
-    @pl.when(jnp.logical_not(odd))
-    def _():
-        bulk[0][2].start()
-
-    for k in range(1, n_area - 1):
-
-        @pl.when(k >= me)
-        def _():
-            for copy in bulk[k][::2]:
-                copy.start()
-
-    for k in range(1, n_area - 1):
-
-        @pl.when((k < me) & jnp.logical_not(held))
-        def _():
-            bulk[k][0].start()
 
     @pl.when(odd)
     def _():

time: 15.8 us -> 15.8 us (level)
  no operation moved by 1% of the time
where the time goes in v7:
time: 15.8 us; the launch traced here: 15.6 us
  Pallas kernels  13 us (82%)
  between operations  2.58 us (16%)
    pallas_call x1, Pallas kernels, body(): pl.pallas_call(functools.partial(kernel, n_area, n_scen), out_shape=(pltp...  12.3 us
    pallas_call x1, Pallas kernels, body(): pl.pallas_call(place, out_shape=tuple((jax.ShapeDtypeStruct(x.shape, x.dt...  0.75 us

profile of v7, /device:TPU:14, one launch (start us, length us, event | category | flops | bytes accessed | tf_op | source)
XLA Modules:
  0.0 15.6 jit_solution(9111244765918041593)
XLA Ops:
  2.6 12.3 %shard_map.121 = (f32[1,16,128]{2,1,0:T(8,128)S(1)}, f32[1,128,512]{2,1,0:T(8,128)S(1)}, f32[1,32,512]{2,1,0:T(8,128)S(1)}) custom-call(f32[32]{0:T(128)} %raw_hbm.1, s32[1,4]{1,0:T(1,128)} %near_hbm.1, s32[1]{0:T(128)S(6)} %copy.13.live_hbm, f32[1,4]{1,0:T(1,128)} %gain_hbm.1, s32[1]{0:T(128)S(6)} %copy.14.plants_hbm, s32[1]{0:T(128)S(6)} %copy.15.inner_hbm, ...), custom_call_target="tpu_custom_call" | custom-call | tf_op jit(solution)/shard_map/pallas_call | solution.py:468
  14.8 0.7 %shard_map.122 = (f32[1,16,128]{2,1,0:T(8,128)}, f32[1,128,512]{2,1,0:T(8,128)}, f32[1,32,512]{2,1,0:T(8,128)}) custom-call(f32[1,16,128]{2,1,0:T(8,128)S(1)} %get-tuple-element.9.refs_0_, f32[1,128,512]{2,1,0:T(8,128)S(1)} %get-tuple-element.10.refs_1_, f32[1,32,512]{2,1,0:T(8,128)S(1)} %get-tuple-element.11.refs_2_), custom_call_target="tpu_custom_call" | custom-call | tf_op jit(solution)/shard_map/pallas_call | solution.py:521
